TPU v7x, 32 devices: a whole 2x2x4 slice. The times are simulated.
32 devices in a mesh: heads: 2 (over x), wide: 16 (over z, y, core).
Axes of the slice: x: 2, y: 2, z: 4, core: 2. Of those that a mesh axis runs over, the one named last changes fastest.
Arguments:
- tokens: bfloat16 [32, 1024, 768], P(('heads', 'wide')), may hold values from -36 to 36
- cotangent: bfloat16 [32, 1024, 768], P(('heads', 'wide')), may hold values from -11 to 11
- lengths: int32 [32], P(('heads', 'wide')), may hold values from 196 to 1024, as said below
- step_count: int32 [1], replicated, may hold values from 2 to 20
- attend_weights: float32 [3, 768, 768], P(None, 'wide', 'heads'), may hold values from -0.21875 to 0.21875
- output_weights: float32 [768, 768], P('heads', 'wide'), may hold values from -7 to 7
- expand_weights: float32 [768, 3072], P('wide', 'heads'), may hold values from -0.21875 to 0.21875
- reduce_weights: float32 [3072, 768], P('heads', 'wide'), may hold values from -1 to 1
- expand_bias: float32 [3072], P(('heads', 'wide')), may hold values from -3 to 3
- norm_gains: float32 [3, 768], P(None, ('heads', 'wide')), may hold values from 0.1 to 1.9
- first_attend: float32 [3, 768, 768], P(None, 'wide', 'heads'), may hold values from -1.25 to 1.25
- first_output: float32 [768, 768], P('heads', 'wide'), may hold values from -0.25 to 0.25
- first_expand: float32 [768, 3072], P('wide', 'heads'), may hold values from -0.875 to 0.875
- first_reduce: float32 [3072, 768], P('heads', 'wide'), may hold values from -2 to 2
- first_bias: float32 [3072], P(('heads', 'wide')), may hold values from -0.875 to 0.875
- first_gains: float32 [3, 768], P(None, ('heads', 'wide')), may hold values from -3 to 3
- second_attend: float32 [3, 768, 768], P(None, 'wide', 'heads'), may hold values from 0.1048576 to 1.703936
- second_output: float32 [768, 768], P('heads', 'wide'), may hold values from 0.0032768 to 0.0524288
- second_expand: float32 [768, 3072], P('wide', 'heads'), may hold values from 0.0458752 to 0.753664
- second_reduce: float32 [3072, 768], P('heads', 'wide'), may hold values from 0.2195456 to 3.60448
- second_bias: float32 [3072], P(('heads', 'wide')), may hold values from 0.0458752 to 0.753664
- second_gains: float32 [3, 768], P(None, ('heads', 'wide')), may hold values from 0.524288 to 8.192
- average_attend: float32 [3, 768, 768], P(None, 'wide', 'heads'), may hold values from -0.21875 to 0.21875
- average_output: float32 [768, 768], P('heads', 'wide'), may hold values from -1.75 to 1.75
- average_expand: float32 [768, 3072], P('wide', 'heads'), may hold values from -0.21875 to 0.21875
- average_reduce: float32 [3072, 768], P('heads', 'wide'), may hold values from -0.109375 to 0.109375
- average_bias: float32 [3072], P(('heads', 'wide')), may hold values from -3 to 3
- average_gains: float32 [3, 768], P(None, ('heads', 'wide')), may hold values from 0.1 to 1.9
Outputs:
- block_output: float32 [32, 1024, 768], P(('heads', 'wide'))
- token_gradient: float32 [32, 1024, 768], P(('heads', 'wide'))
- gradient_norm: float32 [1], replicated
- clip_attend: float32 [3, 768, 768], P(None, 'wide', 'heads')
- mean_attend: float32 [3, 768, 768], P(None, 'wide', 'heads')
- square_attend: float32 [3, 768, 768], P(None, 'wide', 'heads')
- weight_attend: float32 [3, 768, 768], P(None, 'wide', 'heads')
- smooth_attend: float32 [3, 768, 768], P(None, 'wide', 'heads')
- clip_output: float32 [768, 768], P('heads', 'wide')
- mean_output: float32 [768, 768], P('heads', 'wide')
- square_output: float32 [768, 768], P('heads', 'wide')
- weight_output: float32 [768, 768], P('heads', 'wide')
- smooth_output: float32 [768, 768], P('heads', 'wide')
- clip_expand: float32 [768, 3072], P('wide', 'heads')
- mean_expand: float32 [768, 3072], P('wide', 'heads')
- square_expand: float32 [768, 3072], P('wide', 'heads')
- weight_expand: float32 [768, 3072], P('wide', 'heads')
- smooth_expand: float32 [768, 3072], P('wide', 'heads')
- clip_reduce: float32 [3072, 768], P('heads', 'wide')
- mean_reduce: float32 [3072, 768], P('heads', 'wide')
- square_reduce: float32 [3072, 768], P('heads', 'wide')
- weight_reduce: float32 [3072, 768], P('heads', 'wide')
- smooth_reduce: float32 [3072, 768], P('heads', 'wide')
- clip_bias: float32 [3072], P(('heads', 'wide'))
- mean_bias: float32 [3072], P(('heads', 'wide'))
- square_bias: float32 [3072], P(('heads', 'wide'))
- weight_bias: float32 [3072], P(('heads', 'wide'))
- smooth_bias: float32 [3072], P(('heads', 'wide'))
- clip_gains: float32 [3, 768], P(None, ('heads', 'wide'))
- mean_gains: float32 [3, 768], P(None, ('heads', 'wide'))
- square_gains: float32 [3, 768], P(None, ('heads', 'wide'))
- weight_gains: float32 [3, 768], P(None, ('heads', 'wide'))
- smooth_gains: float32 [3, 768], P(None, ('heads', 'wide'))
Inputs may be any that keep to these rules, and one draw needn't show every extreme that they name: `lengths`: each image has 1024 * 196 // 1024 (at least 1), 576 or 1024 valid tokens; image 0 has 1024, image 1 the fewest.
All inputs are finite; a program needn't handle non-finite values.
Results may differ from a plain program's by a relative error of at most 0.011.
Values may be sent and summed in bfloat16 or wider, within the bound.
A program may use at most 192 MiB of HBM per device.

v0:
```python
from functools import partial
import math

import jax
import jax.numpy as jnp
from jax import lax
from jax.sharding import PartitionSpec as P

D = 768
HEAD_DIM = 64
FF = 3072


NORM_EPS = 1e-06
MASKED = -1e30
BETA_FIRST = 0.9
BETA_SECOND = 0.95
AVERAGE_CAP = 0.9999
ADAM_EPS = 1e-08
RATES = (0.03, 0.2, 0.03, 0.015, 0.3, 0.3)
DECAYS = (0.05, 0.05, 0.05, 0.05, 0.0, 0.0)


def norm_parts(values):
    center = values - jnp.mean(values, axis=-1, keepdims=True)
    inverse = lax.rsqrt(jnp.mean(center * center, axis=-1, keepdims=True) + NORM_EPS)
    return (center * inverse, inverse)


def norm_back(upstream, normal, inverse):
    return inverse * (
        upstream
        - jnp.mean(upstream, axis=-1, keepdims=True)
        - normal * jnp.mean(upstream * normal, axis=-1, keepdims=True)
    )


def exact_gelu(values):
    return jax.nn.gelu(values, approximate=False)


def heads_first(values, image_count, head_count):
    slot_count = values.shape[0] // image_count
    head_width = values.shape[1] // head_count
    shaped = values.reshape(image_count, slot_count, head_count, head_width)
    return jnp.transpose(shaped, (0, 2, 1, 3)).reshape(
        image_count * head_count, slot_count, head_width
    )


def tokens_first(values, image_count, head_count):
    slot_count, head_width = (values.shape[1], values.shape[2])
    shaped = values.reshape(image_count, head_count, slot_count, head_width)
    return jnp.transpose(shaped, (0, 2, 1, 3)).reshape(
        image_count * slot_count, head_count * head_width
    )


def block_scores(queries, key_rows, valid_keys, score_scale):
    scores = (
        jnp.einsum("qd,kd->qk", queries, key_rows, preferred_element_type=jnp.float32) * score_scale
    )
    return jnp.where(valid_keys[None, :] > 0, scores, MASKED)


def attend_forward(block_parts, score_scale):
    queries, key_rows, values, valid_keys = block_parts
    scores = block_scores(queries, key_rows, valid_keys, score_scale)
    row_top = jnp.max(scores, axis=-1, keepdims=True)
    expo_scores = jnp.exp(scores - row_top)
    row_total = jnp.sum(expo_scores, axis=-1, keepdims=True)
    probs_low = (expo_scores / row_total).astype(jnp.bfloat16)
    mixed_rows = jnp.dot(probs_low, values, preferred_element_type=jnp.float32)
    return (mixed_rows.astype(jnp.bfloat16), (row_top + jnp.log(row_total))[:, 0])


def attend_backward(block_parts, score_scale):
    queries, key_rows, values, valid_keys, log_total, back_mixed = block_parts
    scores = block_scores(queries, key_rows, valid_keys, score_scale)
    probs = jnp.exp(scores - log_total[:, None])
    back_values = jnp.einsum(
        "qk,qd->kd", probs.astype(jnp.bfloat16), back_mixed, preferred_element_type=jnp.float32
    )
    back_probs = jnp.einsum("qd,kd->qk", back_mixed, values, preferred_element_type=jnp.float32)
    row_inner = jnp.sum(probs * back_probs, axis=-1, keepdims=True)
    back_scores = (probs * (back_probs - row_inner)).astype(jnp.bfloat16)
    back_queries = jnp.dot(back_scores, key_rows, preferred_element_type=jnp.float32) * score_scale
    back_keys = (
        jnp.einsum("qk,qd->kd", back_scores, queries, preferred_element_type=jnp.float32)
        * score_scale
    )
    return (back_queries, back_keys, back_values.astype(jnp.bfloat16))


def branch_forward(normed, valid_mask, weights, query_gain, key_gain):
    attend_w, output_w, expand_w, reduce_w, bias_row = weights
    image_count, slot_count, feature_count = normed.shape
    inner_width = attend_w.shape[2]
    head_count = inner_width // HEAD_DIM
    score_scale = HEAD_DIM ** (-0.5)
    flat_normed = normed.reshape(image_count * slot_count, feature_count)
    projected = jnp.einsum("td,cde->cte", flat_normed, attend_w, preferred_element_type=jnp.float32)
    query_hat, query_inv = norm_parts(projected[0].reshape(-1, head_count, HEAD_DIM))
    key_hat, key_inv = norm_parts(projected[1].reshape(-1, head_count, HEAD_DIM))
    queries = (
        (query_hat * query_gain.reshape(head_count, HEAD_DIM))
        .astype(jnp.bfloat16)
        .reshape(-1, inner_width)
    )
    key_rows = (
        (key_hat * key_gain.reshape(head_count, HEAD_DIM))
        .astype(jnp.bfloat16)
        .reshape(-1, inner_width)
    )
    values = projected[2].astype(jnp.bfloat16)
    query_blocks = heads_first(queries, image_count, head_count)
    key_blocks = heads_first(key_rows, image_count, head_count)
    value_blocks = heads_first(values, image_count, head_count)
    valid_blocks = jnp.repeat(valid_mask, head_count, axis=0)
    mixed_blocks, log_total = lax.map(
        partial(attend_forward, score_scale=score_scale),
        (query_blocks, key_blocks, value_blocks, valid_blocks),
    )
    mixed_heads = tokens_first(mixed_blocks, image_count, head_count)
    pre_act = jnp.dot(flat_normed, expand_w, preferred_element_type=jnp.float32) + bias_row.astype(
        jnp.float32
    )
    hidden = exact_gelu(pre_act).astype(jnp.bfloat16)
    branch_part = jnp.dot(mixed_heads, output_w, preferred_element_type=jnp.float32) + jnp.dot(
        hidden, reduce_w, preferred_element_type=jnp.float32
    )
    saved_state = (
        flat_normed,
        query_blocks,
        key_blocks,
        value_blocks,
        valid_blocks,
        log_total,
        query_hat,
        query_inv,
        key_hat,
        key_inv,
        mixed_heads,
        pre_act,
        hidden,
    )
    return (branch_part.reshape(image_count, slot_count, feature_count), saved_state)


def branch_backward(upstream, weights, saved_state, query_gain, key_gain):
    attend_w, output_w, expand_w, reduce_w, bias_row = weights
    (
        flat_normed,
        query_blocks,
        key_blocks,
        value_blocks,
        valid_blocks,
        log_total,
        query_hat,
        query_inv,
        key_hat,
        key_inv,
        mixed_heads,
        pre_act,
        hidden,
    ) = saved_state
    image_count, slot_count, feature_count = upstream.shape
    inner_width = attend_w.shape[2]
    head_count = inner_width // HEAD_DIM
    score_scale = HEAD_DIM ** (-0.5)
    flat_up = upstream.reshape(-1, feature_count)
    back_output = jnp.einsum("ti,td->id", mixed_heads, flat_up, preferred_element_type=jnp.float32)
    back_mixed = jnp.einsum(
        "td,id->ti", flat_up, output_w, preferred_element_type=jnp.float32
    ).astype(jnp.bfloat16)
    back_reduce = jnp.einsum("tf,td->fd", hidden, flat_up, preferred_element_type=jnp.float32)
    back_hidden = jnp.einsum("td,fd->tf", flat_up, reduce_w, preferred_element_type=jnp.float32)
    back_pre = jax.vjp(exact_gelu, pre_act)[1](back_hidden)[0].astype(jnp.bfloat16)
    back_bias = jnp.sum(back_pre.astype(jnp.float32), axis=0)
    back_expand = jnp.einsum("td,tf->df", flat_normed, back_pre, preferred_element_type=jnp.float32)
    back_qn, back_kn, back_values = lax.map(
        partial(attend_backward, score_scale=score_scale),
        (
            query_blocks,
            key_blocks,
            value_blocks,
            valid_blocks,
            log_total,
            heads_first(back_mixed, image_count, head_count),
        ),
    )
    back_qn = tokens_first(back_qn, image_count, head_count).reshape(-1, head_count, HEAD_DIM)
    back_kn = tokens_first(back_kn, image_count, head_count).reshape(-1, head_count, HEAD_DIM)
    query_gain_grad = jnp.sum(back_qn * query_hat, axis=0).reshape(inner_width)
    key_gain_grad = jnp.sum(back_kn * key_hat, axis=0).reshape(inner_width)
    back_query = (
        norm_back(back_qn * query_gain.reshape(head_count, HEAD_DIM), query_hat, query_inv)
        .reshape(-1, inner_width)
        .astype(jnp.bfloat16)
    )
    back_keyed = (
        norm_back(back_kn * key_gain.reshape(head_count, HEAD_DIM), key_hat, key_inv)
        .reshape(-1, inner_width)
        .astype(jnp.bfloat16)
    )
    back_projected = jnp.stack(
        [back_query, back_keyed, tokens_first(back_values, image_count, head_count)]
    )
    back_attend = jnp.einsum(
        "td,cte->cde", flat_normed, back_projected, preferred_element_type=jnp.float32
    )
    back_normed = jnp.einsum(
        "cte,cde->td", back_projected, attend_w, preferred_element_type=jnp.float32
    )
    back_normed = back_normed + jnp.einsum(
        "tf,df->td", back_pre, expand_w, preferred_element_type=jnp.float32
    )
    weight_parts = (back_attend, back_output, back_expand, back_reduce, back_bias)
    return (
        weight_parts,
        jnp.stack([query_gain_grad, key_gain_grad]),
        back_normed.reshape(image_count, slot_count, feature_count),
    )


def optimizer_update(
    weight, raw_grad, factor, first, second, average, rate, decay, first_fix, second_fix, keep
):
    clipped = raw_grad * factor
    first_new = BETA_FIRST * first + (1.0 - BETA_FIRST) * clipped
    second_new = BETA_SECOND * second + (1.0 - BETA_SECOND) * clipped * clipped
    direction = first_new / first_fix / (jnp.sqrt(second_new / second_fix) + ADAM_EPS)
    weight_new = weight - rate * (direction + decay * weight)
    average_new = keep * average + (1.0 - keep) * weight_new
    return (clipped, first_new, second_new, weight_new, average_new)


def body(
    tokens,
    cotangent,
    lengths,
    step_count,
    attend_weights,
    output_weights,
    expand_weights,
    reduce_weights,
    expand_bias,
    norm_gains,
    first_attend,
    first_output,
    first_expand,
    first_reduce,
    first_bias,
    first_gains,
    second_attend,
    second_output,
    second_expand,
    second_reduce,
    second_bias,
    second_gains,
    average_attend,
    average_output,
    average_expand,
    average_reduce,
    average_bias,
    average_gains,
):
    gains_whole = lax.all_gather(norm_gains, ("heads", "wide"), axis=1, tiled=True)
    image_count, slot_count, feature_count = tokens.shape
    positions = lax.broadcasted_iota(jnp.int32, (image_count, slot_count), 1)
    valid_own = (positions < lengths[:, None]).astype(jnp.float32)
    inputs = tokens.astype(jnp.float32)
    input_hat, input_inv = norm_parts(inputs)
    normed_own = (input_hat * gains_whole[0]).astype(jnp.bfloat16)
    group_weights = (
        lax.all_gather(attend_weights.astype(jnp.bfloat16), "wide", axis=1, tiled=True),
        lax.all_gather(output_weights.astype(jnp.bfloat16), "wide", axis=1, tiled=True),
        lax.all_gather(expand_weights.astype(jnp.bfloat16), "wide", axis=0, tiled=True),
        lax.all_gather(reduce_weights.astype(jnp.bfloat16), "wide", axis=1, tiled=True),
        lax.all_gather(expand_bias.astype(jnp.bfloat16), "wide", axis=0, tiled=True),
    )
    work_normed, valid_low = (
        lax.all_gather(normed_own, "heads", axis=0, tiled=True),
        lax.all_gather(valid_own.astype(jnp.bfloat16), "heads", axis=0, tiled=True),
    )
    work_valid = valid_low.astype(jnp.float32)
    offset = lax.axis_index("heads") * group_weights[0].shape[2]
    inner_width = group_weights[0].shape[2]
    query_gain = lax.dynamic_slice_in_dim(gains_whole[1], offset, inner_width)
    key_gain = lax.dynamic_slice_in_dim(gains_whole[2], offset, inner_width)
    branch_part, saved_state = branch_forward(
        work_normed, work_valid, group_weights, query_gain, key_gain
    )
    update = lax.psum_scatter(
        branch_part.astype(jnp.bfloat16), "heads", scatter_dimension=0, tiled=True
    ).astype(jnp.float32)
    block_output = inputs + update
    upstream_own = cotangent * valid_own.astype(jnp.bfloat16)[:, :, None]
    upstream = lax.all_gather(upstream_own, "heads", axis=0, tiled=True)
    weight_parts, gain_rows, back_normed = branch_backward(
        upstream, group_weights, saved_state, query_gain, key_gain
    )
    back_own = lax.psum_scatter(
        back_normed.astype(jnp.bfloat16), "heads", scatter_dimension=0, tiled=True
    ).astype(jnp.float32)
    token_gradient = upstream_own.astype(jnp.float32) + norm_back(
        back_own * gains_whole[0], input_hat, input_inv
    )
    weight_grads = (
        lax.psum_scatter(weight_parts[0], "wide", scatter_dimension=1, tiled=True),
        lax.psum_scatter(weight_parts[1], "wide", scatter_dimension=1, tiled=True),
        lax.psum_scatter(weight_parts[2], "wide", scatter_dimension=0, tiled=True),
        lax.psum_scatter(weight_parts[3], "wide", scatter_dimension=1, tiled=True),
        lax.psum_scatter(weight_parts[4], "wide", scatter_dimension=0, tiled=True),
    )
    norm_row = jnp.sum((back_own * input_hat).reshape(-1, feature_count), axis=0)
    head_rows = lax.dynamic_update_slice(
        jnp.zeros((2, feature_count), jnp.float32), gain_rows, (0, offset)
    )
    gains_partial = jnp.concatenate([norm_row[None, :], head_rows], axis=0)
    weight_squares = jnp.sum(jnp.stack([jnp.sum(entry * entry) for entry in weight_grads]))
    gains_grad = lax.psum_scatter(gains_partial, ("heads", "wide"), scatter_dimension=1, tiled=True)
    total_squares = lax.psum(weight_squares + jnp.sum(gains_grad * gains_grad), ("heads", "wide"))
    grad_norm = jnp.sqrt(total_squares)
    tokens_all = image_count * slot_count * lax.axis_size("heads") * lax.axis_size("wide")
    limit = 0.02 * math.sqrt(tokens_all * D * FF)
    factor = jnp.minimum(1.0, limit / grad_norm)
    step_float = step_count[0].astype(jnp.float32)
    first_fix = 1.0 - jnp.power(BETA_FIRST, step_float)
    second_fix = 1.0 - jnp.power(BETA_SECOND, step_float)
    keep = jnp.minimum(AVERAGE_CAP, (1.0 + step_float) / (10.0 + step_float))
    masters = (
        attend_weights,
        output_weights,
        expand_weights,
        reduce_weights,
        expand_bias,
        norm_gains,
    )
    raw_grads = (
        weight_grads[0],
        weight_grads[1],
        weight_grads[2],
        weight_grads[3],
        weight_grads[4],
        gains_grad,
    )
    firsts = (first_attend, first_output, first_expand, first_reduce, first_bias, first_gains)
    seconds = (
        second_attend,
        second_output,
        second_expand,
        second_reduce,
        second_bias,
        second_gains,
    )
    averages = (
        average_attend,
        average_output,
        average_expand,
        average_reduce,
        average_bias,
        average_gains,
    )
    updated = [
        optimizer_update(
            masters[index],
            raw_grads[index],
            factor,
            firsts[index],
            seconds[index],
            averages[index],
            RATES[index],
            DECAYS[index],
            first_fix,
            second_fix,
            keep,
        )
        for index in range(6)
    ]
    attend_new, output_new, expand_new, reduce_new, bias_new, gains_new = updated
    return (
        block_output,
        token_gradient,
        grad_norm.reshape(1),
        attend_new[0],
        attend_new[1],
        attend_new[2],
        attend_new[3],
        attend_new[4],
        output_new[0],
        output_new[1],
        output_new[2],
        output_new[3],
        output_new[4],
        expand_new[0],
        expand_new[1],
        expand_new[2],
        expand_new[3],
        expand_new[4],
        reduce_new[0],
        reduce_new[1],
        reduce_new[2],
        reduce_new[3],
        reduce_new[4],
        bias_new[0],
        bias_new[1],
        bias_new[2],
        bias_new[3],
        bias_new[4],
        gains_new[0],
        gains_new[1],
        gains_new[2],
        gains_new[3],
        gains_new[4],
    )


def solution(mesh):
    return jax.shard_map(
        body,
        mesh=mesh,
        in_specs=(
            P(("heads", "wide"), None, None),
            P(("heads", "wide"), None, None),
            P(("heads", "wide")),
            P(),
            P(None, "wide", "heads"),
            P("heads", "wide"),
            P("wide", "heads"),
            P("heads", "wide"),
            P(("heads", "wide")),
            P(None, ("heads", "wide")),
            P(None, "wide", "heads"),
            P("heads", "wide"),
            P("wide", "heads"),
            P("heads", "wide"),
            P(("heads", "wide")),
            P(None, ("heads", "wide")),
            P(None, "wide", "heads"),
            P("heads", "wide"),
            P("wide", "heads"),
            P("heads", "wide"),
            P(("heads", "wide")),
            P(None, ("heads", "wide")),
            P(None, "wide", "heads"),
            P("heads", "wide"),
            P("wide", "heads"),
            P("heads", "wide"),
            P(("heads", "wide")),
            P(None, ("heads", "wide")),
        ),
        out_specs=(
            P(("heads", "wide"), None, None),
            P(("heads", "wide"), None, None),
            P(),
            P(None, "wide", "heads"),
            P(None, "wide", "heads"),
            P(None, "wide", "heads"),
            P(None, "wide", "heads"),
            P(None, "wide", "heads"),
            P("heads", "wide"),
            P("heads", "wide"),
            P("heads", "wide"),
            P("heads", "wide"),
            P("heads", "wide"),
            P("wide", "heads"),
            P("wide", "heads"),
            P("wide", "heads"),
            P("wide", "heads"),
            P("wide", "heads"),
            P("heads", "wide"),
            P("heads", "wide"),
            P("heads", "wide"),
            P("heads", "wide"),
            P("heads", "wide"),
            P(("heads", "wide")),
            P(("heads", "wide")),
            P(("heads", "wide")),
            P(("heads", "wide")),
            P(("heads", "wide")),
            P(None, ("heads", "wide")),
            P(None, ("heads", "wide")),
            P(None, ("heads", "wide")),
            P(None, ("heads", "wide")),
            P(None, ("heads", "wide")),
        ),
        check_vma=False,
    )
```

profile of v0, /device:TPU:0, one launch (start us, length us, event | category | flops | bytes accessed | tf_op | source)
XLA Modules:
  0.0 1031.5 jit_solution(1995139888648216300)
XLA Ops:
  11.5 44.1 %all-gather.1 = f32[32,24,3]{1,2,0:T(4,128)S(1)} all-gather(f32[1,24,3]{1,2,0:T(4,128)S(1)} %bitcast.310), channel_id=1, replica_groups=mesh['heads'=2,'wide'=16] {'heads','wide'}, dimensions={0}, use_global_device_ids=true | all-gather | bytes 9504 | tf_op jit(solution)/shard_map/all_gather | solution.py:268
  61.6 4.3 all-gather
  66.6 19.0 %all_gather.31 = bf16[384,768]{0,1:T(8,128)(2,1)S(1)} all-gather(bf16[384,48]{0,1:T(8,128)(2,1)S(1)} %convert_element_type.144), channel_id=1, replica_groups=mesh['heads'=2,'wide'=16] {'wide'}, dimensions={1}, use_global_device_ids=true | all-gather | bytes 626688 | tf_op jit(solution)/shard_map/all_gather | solution.py:277
  87.2 31.2 %all-reduce = bf16[1536]{0:T(1024)(128)(2,1)S(1)} all-reduce(bf16[1536]{0:T(1024)(128)(2,1)S(1)} %dynamic-update-slice), channel_id=1, replica_groups=mesh['heads'=2,'wide'=16] {'wide'}, use_global_device_ids=true, to_apply=%add | all-reduce | flops 1536 | bytes 6144
  128.4 20.7 %all-gather.10.cloned.1.call-done = bf16[3,768,384]{2,1,0:T(8,128)(2,1)} async-done(((bf16[3,48,384]{2,1,0:T(8,128)(2,1)}), bf16[3,768,384]{2,1,0:T(8,128)(2,1)}) %all-gather.10.cloned.1.call-update) | async-done | bytes 1769488 | tf_op jit(solution)/shard_map/all_gather | solution.py:276
  149.1 6.5 convolution_bitcast_fusion
  165.4 5.6 reshape_squeeze.12
  184.9 5.6 copy.146
  194.8 5.5 copy.145
  204.1 5.9 copy.147
  211.3 133.1 %while.26 = (s32[]{:T(128)}, bf16[12,1024,64]{1,2,0:T(8,128)(2,1)}, f32[12,1024]{1,0:T(8,128)}, f32[12,1024]{1,0:T(8,128)}, bf16[12,1024,64]{2,1,0:T(8,128)(2,1)...) while((s32[]{:T(128)}, bf16[12,1024,64]{1,2,0:T(8,128)(2,1)}, ...), condition=%wide.region_9.10_spmd, body=%wide.region_6.9_spmd.sunk | while | flops 281083904 | bytes 30328960 | solution.py:120
  218.3 4.4 fusion.154
  229.6 4.1 fusion.154
  240.7 4.1 fusion.154
  251.8 4.1 fusion.154
  262.9 4.1 fusion.154
  273.9 4.1 fusion.154
  285.0 4.1 fusion.154
  296.1 4.1 fusion.154
  307.1 4.1 fusion.154
  318.2 4.1 fusion.154
  329.3 4.1 fusion.154
  340.3 4.1 fusion.154
  345.8 177.6 %while.27 = (s32[]{:T(128)}, f32[12,1024,64]{1,2,0:T(8,128)}, f32[12,1024,64]{1,2,0:T(8,128)}, bf16[12,1024,64]{1,2,0:T(8,128)(2,1)}, f32[12,1024]{1,0:T(8,128)}...) while((s32[]{:T(128)}, f32[12,1024,64]{1,2,0:T(8,128)}, ...), condition=%wide.region_13.14_spmd, body=%wide.region_11.13_spmd.sunk | while | flops 687013888 | bytes 33989748 | solution.py:181
  531.2 11.6 %multiply_reduce_fusion.1 = (f32[6,64]{1,0:T(8,128)}, f32[2,1024,6]{1,0,2:T(2,128)}, f32[2,1024,6]{1,0,2:T(2,128)}) fusion(f32[2,1024,6]{1,0,2:T(2,128)} %rsqrt.36, f32[2,1024,6,64]{1,0,3,2:T(2,128)} %reshape_squeeze.12, f32[2,1024,6]{1,0,2:T(2,128)S(1)} %div.147, f32[2,6,1024,64]{2,3,1,0:T(8,128)} %bitcast.285, f32[6,64]{1,0:T(8,128)S(1)} %mul.634), kind=kLoop, calls=%fused_computation.121 | loop fusion | flops 6266496 | bytes 6491136 | tf_op jit(solution)/shard_map/reduce_sum | solution.py:195
  542.9 11.2 %multiply_reduce_fusion.2 = (f32[6,64]{1,0:T(8,128)}, f32[2,1024,6]{1,0,2:T(2,128)S(1)}, f32[2,1024,6]{1,0,2:T(2,128)S(1)}) fusion(f32[2,1024,6]{1,0,2:T(2,128)} %rsqrt.34, f32[2,1024,6,64]{1,0,3,2:T(2,128)S(1)} %copy-done.3, f32[2,1024,6]{1,0,2:T(2,128)S(1)} %div.144, f32[2,6,1024,64]{2,3,1,0:T(8,128)} %bitcast.283, f32[6,64]{1,0:T(8,128)S(1)} %mul.628), kind=kLoop, calls=%fused_computation.122 | loop fusion | flops 6266496 | bytes 6491136 | tf_op jit(solution)/shard_map/reduce_sum | solution.py:194
  554.1 4.1 copy.187
  558.2 4.1 copy.186
  563.8 4.3 reshape_reshape.8
  568.0 5.8 reshape_reshape.9
  573.9 4.2 copy.188
  581.9 4.9 fusion.80
  592.4 4.0 copy.156
  597.0 35.5 %multiply_convert_fusion.1 = (bf16[2048,1536]{1,0:T(8,128)(2,1)}, f32[2048,1536]{1,0:T(8,128)}, f32[2048,1536]{1,0:T(8,128)}) fusion(f32[1536]{0:T(1024)S(1)} %copy-done.47, bf16[2048,768]{1,0:T(8,128)(2,1)} %bitcast.316, bf16[768,1536]{1,0:T(8,128)(2,1)} %all-gather.12.cloned.1.call-done), kind=kOutput, calls=%fused_computation.66 | convolution fusion | flops 5039456256 | bytes 36968448 | tf_op jit(solution)/shard_map/dot_general | solution.py:125
  632.6 16.5 %convert_reduce_fusion = (f32[1536]{0:T(1024)S(1)}, bf16[2048,1536]{1,0:T(8,128)(2,1)}) fusion(f32[2048,1536]{1,0:T(8,128)} %get-tuple-element.368, bf16[2048,768]{1,0:T(8,128)(2,1)S(1)} %bitcast.313, bf16[1536,768]{0,1:T(8,128)(2,1)} %all-gather.14.cloned.1.call-done, f32[2048,1536]{1,0:T(8,128)} %get-tuple-element.384, f32[1536]{0:T(1024)S(1)} %copy-done.47), kind=kOutput, calls=%fused_computation.64 | convolution fusion | flops 4885314048 | bytes 36974592 | tf_op jit(solution)/shard_map/td,fd->tf/dot_general | solution.py:177
  649.1 7.3 fusion.107
  656.5 5.9 fusion.63
  662.5 9.7 fusion.109
  672.2 9.5 fusion.110
  681.9 8.0 fusion.106
  696.3 33.1 %all-reduce.2 = f32[1536]{0:T(1024)S(1)} all-reduce(f32[1536]{0:T(1024)S(1)} %get-tuple-element.385), channel_id=8, replica_groups=mesh['heads'=2,'wide'=16] {'wide'}, use_global_device_ids=true, to_apply=%region_30.31.clone | all-reduce | flops 1536 | bytes 12288
  734.6 31.6 %reduce-scatter.9.cloned.1.call-done = bf16[1,1024,768]{2,1,0:T(8,128)(2,1)} async-done(((bf16[2,1024,768]{2,1,0:T(8,128)(2,1)}), bf16[1,1024,768]{2,1,0:T(8,128)(2,1)}) %reduce-scatter.9.cloned.1.call-update) | async-done | bytes 1572880 | tf_op jit(solution)/shard_map/reduce_scatter | solution.py:303
  769.3 39.6 %all-reduce.3 = f32[3,768]{1,0:T(4,128)S(1)} all-reduce(f32[3,768]{1,0:T(4,128)S(1)} %pad_maximum_fusion.3), channel_id=9, replica_groups=mesh['heads'=2,'wide'=16] {'heads','wide'}, use_global_device_ids=true, to_apply=%region_35.36.clone | all-reduce | flops 2304 | bytes 18432
  809.6 37.2 %reduce-scatter.13.cloned.1.call-done = f32[48,1536]{1,0:T(8,128)} async-done(((f32[768,1536]{1,0:T(8,128)}), f32[48,1536]{1,0:T(8,128)}) %reduce-scatter.13.cloned.1.call-update) | async-done | bytes 294928 | tf_op jit(solution)/shard_map/reduce_scatter | solution.py:312
  849.1 76.0 %reduce-scatter.15.cloned.1.call-done = f32[1536,48]{0,1:T(8,128)} async-done(((f32[1536,768]{0,1:T(8,128)}), f32[1536,48]{0,1:T(8,128)}) %reduce-scatter.15.cloned.1.call-update) | async-done | bytes 294928 | tf_op jit(solution)/shard_map/reduce_scatter | solution.py:313
  928.8 41.7 %reduce-scatter.7.cloned.1.call-done = bf16[1,1024,768]{2,1,0:T(8,128)(2,1)} async-done(((bf16[2,1024,768]{2,1,0:T(8,128)(2,1)}), bf16[1,1024,768]{2,1,0:T(8,128)(2,1)}) %reduce-scatter.7.cloned.1.call-update) | async-done | bytes 1572880 | tf_op jit(solution)/shard_map/reduce_scatter | solution.py:294
  970.4 4.8 fusion.74
  975.3 39.4 %psum.7 = f32[]{:T(128)} all-reduce(f32[]{:T(128)S(6)} %add.221), channel_id=1, replica_groups=mesh['heads'=2,'wide'=16] {'heads','wide'}, use_global_device_ids=true, to_apply=%region_37.38 | all-reduce | flops 1 | bytes 8 | tf_op jit(solution)/shard_map/psum | solution.py:323
  (417 shorter events, 358.0 us)
Async XLA Ops:
  7.2 48.5 %copy-start.1 = (bf16[1,1024,768]{2,1,0:T(8,128)(2,1)S(1)}, bf16[1,1024,768]{2,1,0:T(8,128)(2,1)}, u32[]{:S(2)}) copy-start(bf16[1,1024,768]{2,1,0:T(8,128)(2,1)} %param.32) | copy-start | bytes 4718596
  7.2 111.7 %all-gather.16.cloned.1.call-start = ((), (), s32[]{:S(2)}) async-start(), calls=%async_computation.10 | async-start | bytes 4718592 | tf_op jit(solution)/shard_map/all_gather | solution.py:299
  11.4 116.9 %all-gather.8.cloned.1.call-start = ((), (), s32[]{:S(2)}) async-start(), calls=%async_computation.5 | async-start | bytes 4718592 | tf_op jit(solution)/shard_map/all_gather | solution.py:283
  57.3 9.2 copy-start.24
  57.3 28.3 %copy-start.52 = (f32[96]{0:T(128)S(1)}, f32[96]{0:T(128)}, u32[]{:S(2)}) copy-start(f32[96]{0:T(128)} %param.40) | copy-start | bytes 1156
  57.3 28.3 %copy-start.51 = (u32[32]{0:T(128)S(1)}, u32[32]{0:T(128)}, u32[]{:S(2)}) copy-start(u32[32]{0:T(128)} %constant.223) | copy-start | bytes 388
  59.0 90.1 %all-gather.10.cloned.1.call-start = ((), (), s32[]{:S(2)}) async-start(), calls=%async_computation.6 | async-start | bytes 1880064 | tf_op jit(solution)/shard_map/all_gather | solution.py:276
  59.8 536.7 %all-gather.12.cloned.1.call-start = ((), (), s32[]{:S(2)}) async-start(), calls=%async_computation.7 | async-start | bytes 2506752 | tf_op jit(solution)/shard_map/all_gather | solution.py:278
  60.5 572.0 %all-gather.14.cloned.1.call-start = ((), (), s32[]{:S(2)}) async-start(), calls=%async_computation.8 | async-start | bytes 2506752 | tf_op jit(solution)/shard_map/all_gather | solution.py:279
  61.3 668.7 %reduce-scatter.11.cloned.1.call-start = ((), (), s32[]{:S(2)}) async-start(), calls=%async_computation.12 | async-start | bytes 1253376 | tf_op jit(solution)/shard_map/reduce_scatter | solution.py:311
  85.6 33.4 %copy-start.11 = (bf16[384,768]{0,1:T(8,128)(2,1)}, bf16[384,768]{0,1:T(8,128)(2,1)S(1)}, u32[]{:S(2)}) copy-start(bf16[384,768]{0,1:T(8,128)(2,1)S(1)} %all_gather.31) | copy-start | bytes 1769476
  176.3 5.0 copy-start.4
  184.9 6.3 copy-start.3
  542.8 188.7 %all-reduce.6.cloned.1.call-start = ((), (), s32[]{:S(2)}) async-start(), calls=%async_computation.15 | async-start | bytes 9437184
  542.8 11.2 %copy-start.6 = (f32[12,1024,64]{1,2,0:T(8,128)S(1)}, f32[12,1024,64]{1,2,0:T(8,128)}, u32[]{:S(2)}) copy-start(f32[12,1024,64]{1,2,0:T(8,128)} %get-tuple-element.127) | copy-start | bytes 9437188
  581.9 6.6 copy-start.17
  581.9 6.6 copy-start.59
  596.4 169.8 %reduce-scatter.9.cloned.1.call-start = ((), (), s32[]{:S(2)}) async-start(), calls=%async_computation.11 | async-start | bytes 4718592 | tf_op jit(solution)/shard_map/reduce_scatter | solution.py:303
  597.0 35.5 %copy-start.58 = (bf16[2,1024,768]{2,1,0:T(8,128)(2,1)S(1)}, bf16[2,1024,768]{2,1,0:T(8,128)(2,1)}, u32[]{:S(2)}) copy-start(bf16[2,1024,768]{2,1,0:T(8,128)(2,1)} %all-gather.16.cloned.1.call-done) | copy-start | bytes 9437188
  632.6 16.5 %copy-start.60 = (bf16[768,1536]{1,0:T(8,128)(2,1)S(1)}, bf16[768,1536]{1,0:T(8,128)(2,1)}, u32[]{:S(2)}) copy-start(bf16[768,1536]{1,0:T(8,128)(2,1)} %all-gather.12.cloned.1.call-done) | copy-start | bytes 7077892
  649.1 7.4 copy-start.14
  649.1 7.4 copy-start.16
  649.1 7.4 copy-start.18
  649.1 7.4 copy-start.61
  662.4 184.3 %reduce-scatter.13.cloned.1.call-start = ((), (), s32[]{:S(2)}) async-start(), calls=%async_computation.13 | async-start | bytes 5013504 | tf_op jit(solution)/shard_map/reduce_scatter | solution.py:312
  672.2 252.9 %reduce-scatter.15.cloned.1.call-start = ((), (), s32[]{:S(2)}) async-start(), calls=%async_computation.14 | async-start | bytes 5013504 | tf_op jit(solution)/shard_map/reduce_scatter | solution.py:313
  681.8 8.1 copy-start.10
  681.8 8.1 copy-start.12
  681.8 288.6 %reduce-scatter.7.cloned.1.call-start = ((), (), s32[]{:S(2)}) async-start(), calls=%async_computation.9 | async-start | bytes 4718592 | tf_op jit(solution)/shard_map/reduce_scatter | solution.py:294
  693.5 72.7 %copy-start.2 = (bf16[1,1024,768]{2,1,0:T(8,128)(2,1)S(1)}, bf16[1,1024,768]{2,1,0:T(8,128)(2,1)}, u32[]{:S(2)}) copy-start(bf16[1,1024,768]{2,1,0:T(8,128)(2,1)} %param.32) | copy-start | bytes 4718596
  693.5 72.7 %copy-start.33 = (f32[1024]{0:T(1024)S(1)}, f32[1024]{0:T(1024)}, u32[]{:S(2)}) copy-start(f32[1024]{0:T(1024)} %copy-done.32) | copy-start | bytes 12292
  693.5 72.7 %copy-start.38 = (f32[768]{0:T(1024)S(1)}, f32[768]{0:T(1024)}, u32[]{:S(2)}) copy-start(f32[768]{0:T(1024)} %copy-done.37) | copy-start | bytes 9220
  693.5 72.7 %copy-start.40 = (f32[1024]{0:T(1024)S(1)}, f32[1024]{0:T(1024)}, u32[]{:S(2)}) copy-start(f32[1024]{0:T(1024)} %copy-done.39) | copy-start | bytes 12292
  693.6 276.9 %copy-start.8 = (bf16[1,1024,768]{2,1,0:T(8,128)(2,1)S(1)}, bf16[1,1024,768]{2,1,0:T(8,128)(2,1)}, u32[]{:S(2)}) copy-start(bf16[1,1024,768]{2,1,0:T(8,128)(2,1)} %param.33) | copy-start | bytes 4718596
  693.6 276.9 %copy-start.42 = (bf16[1024]{0:T(1024)(128)(2,1)S(1)}, bf16[1024]{0:T(1024)(128)(2,1)}, u32[]{:S(2)}) copy-start(bf16[1024]{0:T(1024)(128)(2,1)} %copy-done.41) | copy-start | bytes 6148
  928.7 86.7 %copy-start.46 = (f32[3,24]{1,0:T(4,128)S(1)}, f32[3,24]{1,0:T(4,128)}, u32[]{:S(2)}) copy-start(f32[3,24]{1,0:T(4,128)} %param.41) | copy-start | bytes 868
  928.7 86.7 %copy-start.48 = (f32[3,24]{1,0:T(4,128)S(1)}, f32[3,24]{1,0:T(4,128)}, u32[]{:S(2)}) copy-start(f32[3,24]{1,0:T(4,128)} %param.59) | copy-start | bytes 868
  928.7 86.7 %copy-start.49 = (f32[3,24]{1,0:T(4,128)S(1)}, f32[3,24]{1,0:T(4,128)}, u32[]{:S(2)}) copy-start(f32[3,24]{1,0:T(4,128)} %param.53) | copy-start | bytes 868
  928.7 86.7 %copy-start.50 = (f32[3,24]{1,0:T(4,128)S(1)}, f32[3,24]{1,0:T(4,128)}, u32[]{:S(2)}) copy-start(f32[3,24]{1,0:T(4,128)} %param.47) | copy-start | bytes 868
  928.7 87.4 %copy-start.53 = (f32[96]{0:T(128)S(1)}, f32[96]{0:T(128)}, u32[]{:S(2)}) copy-start(f32[96]{0:T(128)} %param.40) | copy-start | bytes 1156
  928.7 87.4 %copy-start.54 = (f32[96]{0:T(128)S(1)}, f32[96]{0:T(128)}, u32[]{:S(2)}) copy-start(f32[96]{0:T(128)} %param.58) | copy-start | bytes 1156
  928.7 87.4 %copy-start.55 = (f32[96]{0:T(128)S(1)}, f32[96]{0:T(128)}, u32[]{:S(2)}) copy-start(f32[96]{0:T(128)} %param.52) | copy-start | bytes 1156
  928.7 87.4 %copy-start.56 = (f32[96]{0:T(128)S(1)}, f32[96]{0:T(128)}, u32[]{:S(2)}) copy-start(f32[96]{0:T(128)} %param.46) | copy-start | bytes 1156
  975.2 46.4 %copy-start.21 = (f32[48,1536]{1,0:T(8,128)S(1)}, f32[48,1536]{1,0:T(8,128)}, u32[]{:S(2)}) copy-start(f32[48,1536]{1,0:T(8,128)} %param.38) | copy-start | bytes 884740
  975.3 46.4 %copy-start.22 = (f32[48,1536]{1,0:T(8,128)S(1)}, f32[48,1536]{1,0:T(8,128)}, u32[]{:S(2)}) copy-start(f32[48,1536]{1,0:T(8,128)} %reduce-scatter.13.cloned.1.call-done) | copy-start | bytes 884740
  975.3 46.4 %copy-start.27 = (f32[48,1536]{1,0:T(8,128)S(1)}, f32[48,1536]{1,0:T(8,128)}, u32[]{:S(2)}) copy-start(f32[48,1536]{1,0:T(8,128)} %param.56) | copy-start | bytes 884740
  975.3 46.4 %copy-start.28 = (f32[48,1536]{1,0:T(8,128)S(1)}, f32[48,1536]{1,0:T(8,128)}, u32[]{:S(2)}) copy-start(f32[48,1536]{1,0:T(8,128)} %param.50) | copy-start | bytes 884740
  975.3 46.4 %copy-start.29 = (f32[48,1536]{1,0:T(8,128)S(1)}, f32[48,1536]{1,0:T(8,128)}, u32[]{:S(2)}) copy-start(f32[48,1536]{1,0:T(8,128)} %param.44) | copy-start | bytes 884740
  (36 other events, 92.9 us)
Sparse Core Ops, SparseCore 0:
  11.6 47.6 all-gather.15
  60.8 44.9 all-gather.7
  108.6 40.3 all-gather.9
  151.8 41.1 all-gather.11
  195.6 40.9 all-gather.13
  542.9 57.0 reduce-scatter.10
  603.6 116.5 all-reduce.5
  723.0 43.1 reduce-scatter.8
  770.6 76.1 reduce-scatter.12
  850.5 74.5 reduce-scatter.14
  928.0 42.3 reduce-scatter.6
where the time goes:
time: 1040 us; the launch traced here: 1030 us
  matrix products  324 us (31%)
  blocking collectives  211 us (20%)
  waiting for transfers between devices  207 us (20%)
  local copies, waits for them, and re-layouts  141 us (14%)
  other arithmetic  123 us (12%)
  between operations  24.7 us (2%)
    unnamed x3, blocking collectives  104 us
    reduce_scatter x1, waiting for transfers between devices, body(): lax.psum_scatter(weight_parts[3], 'wide', scatter_dimension=1, tiled=True)  76 us
    dot_general x12, matrix products, attend_forward(): mixed_rows = jnp.dot(probs_low, values, preferred_element_type=jnp.float32)  49.7 us
    all_gather x1, blocking collectives, body(): lax.all_gather(norm_gains, ('heads', 'wide'), axis=1, tiled=True)  44.1 us
    dot_general x24, matrix products, block_scores(): jnp.einsum('qd,kd->qk', queries, key_rows, preferred_element_type=jnp.flo...  41.9 us
    reduce_scatter x1, waiting for transfers between devices, body(): lax.psum_scatter(branch_part.astype(jnp.bfloat16), 'heads', scatter_dimen...  41.7 us
    psum x1, blocking collectives, body(): lax.psum(weight_squares + jnp.sum(gains_grad * gains_grad), ('heads', 'wi...  39.4 us
    reduce_scatter x1, waiting for transfers between devices, body(): lax.psum_scatter(weight_parts[2], 'wide', scatter_dimension=0, tiled=True)  37.2 us
  transfers between devices with their start and end apart: 11, of which 5 were waited for; matrix products, arithmetic and copies ran while one was open for 52% of the time, Pallas kernels for 0%

commit v1 on v0

v1 whole, which is shorter than its diff:
```python
from functools import partial
import math

import jax
import jax.numpy as jnp
from jax import lax
from jax.experimental import pallas as pl
from jax.experimental.pallas import tpu as pltpu
from jax.sharding import PartitionSpec as P

D = 768
HEADS = 12
HEAD_DIM = 64
FF = 3072
HALF_E = D // 2
HALF_F = FF // 2
PAIR = 128
PAIRS = HALF_E // PAIR
CHUNK = 512
CHUNKS = HALF_F // CHUNK
QUERY_ROWS = 512
BF = jnp.bfloat16
F32 = jnp.float32

NORM_EPS = 1e-06
MASKED = -1e30
BETA_FIRST = 0.9
BETA_SECOND = 0.95
AVERAGE_CAP = 0.9999
ADAM_EPS = 1e-08
RATES = (0.03, 0.2, 0.03, 0.015, 0.3, 0.3)
DECAYS = (0.05, 0.05, 0.05, 0.05, 0.0, 0.0)


def dot(left, right, left_dim, right_dim):
    return lax.dot_general(
        left, right, (((left_dim,), (right_dim,)), ((), ())), preferred_element_type=F32
    )


def row_norm(values):
    center = values - jnp.mean(values, axis=-1, keepdims=True)
    inverse = lax.rsqrt(jnp.mean(center * center, axis=-1, keepdims=True) + NORM_EPS)
    return center * inverse, inverse


def head_mean(values):
    width = values.shape[1]
    row = lax.broadcasted_iota(jnp.int32, (width, width), 0) // HEAD_DIM
    column = lax.broadcasted_iota(jnp.int32, (width, width), 1) // HEAD_DIM
    block = jnp.where(row == column, 1.0 / HEAD_DIM, 0.0).astype(BF)
    high = values.astype(BF)
    rest = (values - high.astype(F32)).astype(BF)
    return dot(high, block, 1, 0) + dot(rest, block, 1, 0)


def head_norm(values):
    center = values - head_mean(values)
    inverse = lax.rsqrt(head_mean(center * center) + NORM_EPS)
    return center * inverse, inverse


def head_norm_back(upstream, normal, inverse):
    return inverse * (upstream - head_mean(upstream) - normal * head_mean(upstream * normal))


def pair_attention(query, keyed, value, back_mixed, key_bias):
    rows = query.shape[0]
    lane = lax.broadcasted_iota(jnp.int32, (rows, PAIR), 1)
    low = lane < HEAD_DIM
    first = lane == 0
    zero = jnp.zeros((rows, PAIR), BF)
    one_lane = jnp.where(first, 1.0, 0.0).astype(BF)
    bias_lane = jnp.where(first, key_bias, 0.0).astype(BF)
    query_wide = jnp.concatenate([query, one_lane], axis=1)
    value_wide = jnp.concatenate([value, jnp.ones((rows, PAIR), BF)], axis=1)
    blocks = rows // QUERY_ROWS
    mixed = [[None] * blocks for _ in range(2)]
    back_query = [[None] * blocks for _ in range(2)]
    back_keyed = None
    back_value = None
    lane_q = lane[:QUERY_ROWS]
    low_q = low[:QUERY_ROWS]
    for head in range(2):
        mine = low if head == 0 else ~low
        mine_q = mine[:QUERY_ROWS]
        key_wide = jnp.concatenate([jnp.where(mine, keyed, zero), bias_lane], axis=1)
        query_mine = jnp.where(mine, query, zero)
        for block in range(blocks):
            cut = slice(block * QUERY_ROWS, (block + 1) * QUERY_ROWS)
            expo = jnp.exp(dot(query_wide[cut], key_wide, 1, 1))
            expo_low = expo.astype(BF)
            sums = dot(expo_low, value_wide, 1, 0)
            inverse = 1.0 / sums[:, PAIR:]
            rows_mixed = sums[:, :PAIR] * inverse
            scaled = jnp.where(mine_q, back_mixed[cut].astype(F32) * inverse, 0.0).astype(BF)
            inner = jnp.sum(rows_mixed * scaled.astype(F32), axis=1, keepdims=True)
            inner_high = inner.astype(BF).astype(F32)
            inner_lanes = jnp.where(
                lane_q == 0, -inner_high, jnp.where(lane_q == 1, inner_high - inner, 0.0)
            ).astype(BF)
            centered = dot(jnp.concatenate([scaled, inner_lanes], axis=1), value_wide, 1, 1)
            back_scores = (expo * centered).astype(BF)
            mixed[head][block] = rows_mixed
            back_query[head][block] = dot(back_scores, keyed, 1, 0)
            add_keyed = dot(query_mine[cut], back_scores, 0, 0)
            add_value = dot(scaled, expo_low, 0, 0)
            back_keyed = add_keyed if back_keyed is None else back_keyed + add_keyed
            back_value = add_value if back_value is None else back_value + add_value
    join = lambda parts: jnp.concatenate(
        [jnp.where(low_q, parts[0][block], parts[1][block]) for block in range(blocks)], axis=0
    )
    return join(mixed).astype(BF), join(back_query), back_keyed.T, back_value.T.astype(BF)


def attention_section(weights_first, weights_second, normed, upstream, query_gain, key_gain, key_bias):
    three = 3 * PAIR
    into = jnp.concatenate([weights_first[:, :three], weights_second[:, :three]], axis=1)
    out = jnp.concatenate([weights_first[:, three:], weights_second[:, three:]], axis=1)
    projected = dot(normed, into, 1, 0)
    back_mixed = dot(upstream, out, 1, 0).astype(BF)
    pick = lambda place: jnp.concatenate(
        [
            projected[:, place * PAIR : (place + 1) * PAIR],
            projected[:, three + place * PAIR : three + (place + 1) * PAIR],
        ],
        axis=1,
    )
    query_hat, query_inv = head_norm(pick(0))
    key_hat, key_inv = head_norm(pick(1))
    query = (query_hat * query_gain).astype(BF)
    keyed = (key_hat * key_gain).astype(BF)
    value = pick(2).astype(BF)
    query = (query.astype(F32) * HEAD_DIM ** (-0.5)).astype(BF)
    parts = [
        pair_attention(
            query[:, cut], keyed[:, cut], value[:, cut], back_mixed[:, cut], key_bias
        )
        for cut in (slice(0, PAIR), slice(PAIR, 2 * PAIR))
    ]
    mixed = jnp.concatenate([parts[0][0], parts[1][0]], axis=1)
    back_qn = jnp.concatenate([parts[0][1], parts[1][1]], axis=1) * HEAD_DIM ** (-0.5)
    back_kn = jnp.concatenate([parts[0][2], parts[1][2]], axis=1)
    query_gain_back = jnp.sum(back_qn * query_hat, axis=0, keepdims=True)
    key_gain_back = jnp.sum(back_kn * key_hat, axis=0, keepdims=True)
    back_query = head_norm_back(back_qn * query_gain, query_hat, query_inv).astype(BF)
    back_keyed = head_norm_back(back_kn * key_gain, key_hat, key_inv).astype(BF)
    back_into = jnp.concatenate(
        [
            back_query[:, :PAIR],
            back_keyed[:, :PAIR],
            parts[0][3],
            back_query[:, PAIR:],
            back_keyed[:, PAIR:],
            parts[1][3],
        ],
        axis=1,
    )
    add_out = dot(mixed, out, 1, 1)
    add_back = dot(back_into, into, 1, 1)
    grad_into = dot(normed, back_into, 0, 0)
    grad_out = dot(upstream, mixed, 0, 0)
    grads = [
        jnp.concatenate(
            [grad_into[:, half * three : (half + 1) * three], grad_out[:, half * PAIR : (half + 1) * PAIR]],
            axis=1,
        )
        for half in range(2)
    ]
    return add_out, add_back, grads, query_gain_back, key_gain_back


def mlp_section(weights, normed, upstream, bias):
    expand = weights[:, :CHUNK]
    reduce = weights[:, CHUNK:]
    pre = dot(normed, expand, 1, 0) + bias
    back_hidden = dot(upstream, reduce, 1, 0)
    phi = 0.5 * (1.0 + lax.erf(pre * math.sqrt(0.5)))
    density = jnp.exp(-0.5 * pre * pre) * (1.0 / math.sqrt(2.0 * math.pi))
    hidden = (pre * phi).astype(BF)
    back_pre = (back_hidden * (phi + pre * density)).astype(BF)
    add_out = dot(hidden, reduce, 1, 1)
    add_back = dot(back_pre, expand, 1, 1)
    grad = jnp.concatenate([dot(normed, back_pre, 0, 0), dot(upstream, hidden, 0, 0)], axis=1)
    return add_out, add_back, grad, jnp.sum(back_pre.astype(F32), axis=0, keepdims=True)


def start_input(
    length_ref, tokens_ref, cotangent_ref, gains_ref, normed_ref, upstream_ref, out_ref, back_ref
):
    place = lax.broadcasted_iota(jnp.int32, (tokens_ref.shape[0], 1), 0)
    inputs = tokens_ref[...].astype(F32)
    input_hat, _ = row_norm(inputs)
    normed_ref[...] = (input_hat * gains_ref[0:1, :]).astype(BF)
    upstream_ref[...] = jnp.where(place < length_ref[0], cotangent_ref[...].astype(F32), 0.0).astype(BF)
    out_ref[...] = inputs
    back_ref[...] = jnp.zeros_like(back_ref)


def finish_input(tokens_ref, gains_ref, upstream_ref, back_ref, gains_back_ref):
    input_hat, input_inv = row_norm(tokens_ref[...].astype(F32))
    back_normed = back_ref[...]
    gains_back_ref[0:1, :] = jnp.sum(back_normed * input_hat, axis=0, keepdims=True)
    scaled = back_normed * gains_ref[0:1, :]
    back_ref[...] = upstream_ref[...].astype(F32) + input_inv * (
        scaled
        - jnp.mean(scaled, axis=-1, keepdims=True)
        - input_hat * jnp.mean(scaled * input_hat, axis=-1, keepdims=True)
    )


def local_kernel(
    length_ref, tokens_ref, cotangent_ref, gains_ref, bias_ref, pair_ref, chunk_ref,
    out_ref, back_ref, grad_pair_ref, grad_chunk_ref, bias_back_ref, gains_back_ref,
    normed_ref, upstream_ref,
):
    index = pl.program_id(0)

    @pl.when(index == 0)
    def _():
        start_input(
            length_ref, tokens_ref, cotangent_ref, gains_ref, normed_ref, upstream_ref, out_ref, back_ref
        )

    is_pair = (index == 0) | (index > 2 * CHUNKS)

    @pl.when(is_pair)
    def _():
        unit = jnp.where(index == 0, 0, index - 2 * CHUNKS)
        starts = [pl.multiple_of(half * HALF_E + unit * PAIR, PAIR) for half in range(2)]
        gain_of = lambda row: jnp.concatenate(
            [gains_ref[row : row + 1, pl.ds(start, PAIR)] for start in starts], axis=1
        )
        place = lax.broadcasted_iota(jnp.int32, (tokens_ref.shape[0], 1), 0)
        add_out, add_back, grads, query_back, key_back = attention_section(
            pair_ref[0, 0], pair_ref[0, 1], normed_ref[...], upstream_ref[...],
            gain_of(1), gain_of(2), jnp.where(place < length_ref[0], 0.0, MASKED),
        )
        out_ref[...] += add_out
        back_ref[...] += add_back
        for half in range(2):
            grad_pair_ref[0, half] = grads[half].astype(BF)
            cut = slice(half * PAIR, (half + 1) * PAIR)
            gains_back_ref[1:2, pl.ds(starts[half], PAIR)] = query_back[:, cut]
            gains_back_ref[2:3, pl.ds(starts[half], PAIR)] = key_back[:, cut]

    @pl.when(~is_pair)
    def _():
        unit = (index - 1) // 2
        half = lax.rem(index - 1, 2)
        start = pl.multiple_of(half * HALF_F + unit * CHUNK, CHUNK)
        add_out, add_back, grad, bias_back = mlp_section(
            chunk_ref[0, 0], normed_ref[...], upstream_ref[...],
            bias_ref[0:1, pl.ds(start, CHUNK)],
        )
        out_ref[...] += add_out
        back_ref[...] += add_back
        grad_chunk_ref[0, 0] = grad.astype(BF)
        bias_back_ref[0:1, pl.ds(start, CHUNK)] = bias_back

    @pl.when(index == PAIRS + 2 * CHUNKS - 1)
    def _():
        finish_input(tokens_ref, gains_ref, upstream_ref, back_ref, gains_back_ref)


def local_block(length, tokens, cotangent, gains, bias, pair_weights, chunk_weights):
    slots = tokens.shape[0]
    steps = PAIRS + 2 * CHUNKS
    whole = lambda shape: pl.BlockSpec(shape, lambda index: (0,) * len(shape))
    pair_at = lambda index: (jnp.maximum(index - 2 * CHUNKS, 0), 0, 0, 0)

    def chunk_at(index):
        flat = jnp.clip(index - 1, 0, 2 * CHUNKS - 1)
        return (flat // 2, lax.rem(flat, 2), 0, 0)

    pair_spec = pl.BlockSpec((1, 2, D, 4 * PAIR), pair_at)
    chunk_spec = pl.BlockSpec((1, 1, D, 2 * CHUNK), chunk_at)
    return pl.pallas_call(
        local_kernel,
        grid=(steps,),
        in_specs=[
            pl.BlockSpec(memory_space=pltpu.SMEM),
            whole((slots, D)), whole((slots, D)), whole((3, D)), whole((1, FF)), pair_spec, chunk_spec,
        ],
        out_specs=[
            whole((slots, D)), whole((slots, D)), pair_spec, chunk_spec, whole((1, FF)), whole((3, D)),
        ],
        out_shape=[
            jax.ShapeDtypeStruct((slots, D), F32),
            jax.ShapeDtypeStruct((slots, D), F32),
            jax.ShapeDtypeStruct((PAIRS, 2, D, 4 * PAIR), BF),
            jax.ShapeDtypeStruct((CHUNKS, 2, D, 2 * CHUNK), BF),
            jax.ShapeDtypeStruct((1, FF), F32),
            jax.ShapeDtypeStruct((3, D), F32),
        ],
        scratch_shapes=[pltpu.VMEM((slots, D), BF), pltpu.VMEM((slots, D), BF)],
        compiler_params=pltpu.CompilerParams(vmem_limit_bytes=60 << 20),
        name="local_block",
    )(length, tokens, cotangent, gains, bias, pair_weights, chunk_weights)


def optimizer_update(
    weight, raw_grad, factor, first, second, average, rate, decay, first_fix, second_fix, keep
):
    clipped = raw_grad * factor
    first_new = BETA_FIRST * first + (1.0 - BETA_FIRST) * clipped
    second_new = BETA_SECOND * second + (1.0 - BETA_SECOND) * clipped * clipped
    direction = first_new / first_fix / (jnp.sqrt(second_new / second_fix) + ADAM_EPS)
    weight_new = weight - rate * (direction + decay * weight)
    average_new = keep * average + (1.0 - keep) * weight_new
    return (clipped, first_new, second_new, weight_new, average_new)


def pack_shards(attend_weights, output_weights, expand_weights, reduce_weights):
    rows = attend_weights.shape[1]
    attend = attend_weights.astype(BF).reshape(3, rows, PAIRS, PAIR)
    attend = jnp.transpose(attend, (2, 1, 0, 3)).reshape(PAIRS, rows, 3 * PAIR)
    output = jnp.transpose(
        output_weights.astype(BF).T.reshape(rows, PAIRS, PAIR), (1, 0, 2)
    )
    expand = jnp.transpose(expand_weights.astype(BF).reshape(rows, CHUNKS, CHUNK), (1, 0, 2))
    reduce = jnp.transpose(reduce_weights.astype(BF).T.reshape(rows, CHUNKS, CHUNK), (1, 0, 2))
    return jnp.concatenate([attend, output], axis=2), jnp.concatenate([expand, reduce], axis=2)


def unpack_shards(pair_grads, chunk_grads):
    rows = pair_grads.shape[1]
    attend = jnp.transpose(
        pair_grads[:, :, : 3 * PAIR].reshape(PAIRS, rows, 3, PAIR), (2, 1, 0, 3)
    ).reshape(3, rows, HALF_E)
    join = lambda part: jnp.transpose(part, (1, 0, 2)).reshape(rows, -1)
    return (
        attend,
        join(pair_grads[:, :, 3 * PAIR :]).T,
        join(chunk_grads[:, :, :CHUNK]),
        join(chunk_grads[:, :, CHUNK:]).T,
    )


def gathered_block(lengths, tokens, cotangent, norm_gains, expand_bias, pair_own, chunk_own):
    both = ("heads", "wide")
    gains = lax.all_gather(norm_gains, both, axis=1, tiled=True)
    bias = lax.all_gather(expand_bias.astype(BF), both, axis=0, tiled=True).astype(F32)
    whole = lambda own: lax.all_gather(
        lax.all_gather(own, "wide", axis=1, tiled=True), "heads", axis=1
    )
    block_output, token_gradient, pair_grads, chunk_grads, bias_back, gains_back = local_block(
        lengths, tokens, cotangent, gains, bias[None, :], whole(pair_own), whole(chunk_own)
    )
    scatter = lambda part: lax.psum_scatter(
        lax.psum_scatter(part, "heads", scatter_dimension=1),
        "wide", scatter_dimension=1, tiled=True,
    ).astype(F32)
    grads = unpack_shards(scatter(pair_grads), scatter(chunk_grads)) + (
        lax.psum_scatter(bias_back[0], both, scatter_dimension=0, tiled=True),
        lax.psum_scatter(gains_back, both, scatter_dimension=1, tiled=True),
    )
    squares = jnp.sum(jnp.stack([jnp.sum(entry * entry) for entry in grads]))
    return block_output, token_gradient, grads, lax.psum(squares, both)


def body(
    tokens, cotangent, lengths, step_count,
    attend_weights, output_weights, expand_weights, reduce_weights, expand_bias, norm_gains,
    *moments,
):
    masters = (
        attend_weights, output_weights, expand_weights, reduce_weights, expand_bias, norm_gains,
    )
    firsts, seconds, averages = moments[:6], moments[6:12], moments[12:]
    pair_own, chunk_own = pack_shards(*masters[:4])
    block_output, token_gradient, grads, total_squares = gathered_block(
        lengths, tokens[0], cotangent[0], norm_gains, expand_bias, pair_own, chunk_own
    )
    grad_norm = jnp.sqrt(total_squares)
    tokens_all = tokens.shape[1] * lax.axis_size("heads") * lax.axis_size("wide")
    limit = 0.02 * math.sqrt(tokens_all * D * FF)
    factor = jnp.minimum(1.0, limit / grad_norm)
    step_float = step_count[0].astype(F32)
    first_fix = 1.0 - jnp.power(BETA_FIRST, step_float)
    second_fix = 1.0 - jnp.power(BETA_SECOND, step_float)
    keep = jnp.minimum(AVERAGE_CAP, (1.0 + step_float) / (10.0 + step_float))
    results = [block_output[None], token_gradient[None], grad_norm.reshape(1)]
    for index in range(6):
        results.extend(
            optimizer_update(
                masters[index], grads[index], factor, firsts[index], seconds[index],
                averages[index], RATES[index], DECAYS[index], first_fix, second_fix, keep,
            )
        )
    return tuple(results)


def solution(mesh):
    both = ("heads", "wide")
    weight_specs = (
        P(None, "wide", "heads"), P("heads", "wide"), P("wide", "heads"), P("heads", "wide"),
        P(both), P(None, both),
    )
    image = P(both, None, None)
    return jax.shard_map(
        body,
        mesh=mesh,
        in_specs=(image, image, P(both), P()) + weight_specs * 4,
        out_specs=(image, image, P()) + tuple(spec for spec in weight_specs for _ in range(5)),
        check_vma=False,
    )
```

time: 1040 us -> 948 us (0.912)
  waiting for transfers between devices: 207 us -> 612 us
  matrix products: 324 us -> 0 us
  local copies, waits for them, and re-layouts: 141 us -> 13.5 us
  Pallas kernels: 0 us -> 112 us
  other arithmetic: 123 us -> 20.8 us
  blocking collectives: 211 us -> 157 us
    dot_general x96 -> x0, matrix products: 324 us -> none  [the longest x12 49.7 us: attend_forward(): mixed_rows = jnp.dot(probs_low, values, preferred_element_type=jnp.float32)]
    unnamed x12 -> x8, waiting for transfers between devices: 0.18 us -> 322 us
    all_gather x5 -> x4, waiting for transfers between devices: 20.7 us -> 200 us  [the longest x2 102 us: gathered_block(): lax.all_gather(lax.all_gather(own, 'wide', axis=1, tiled=True), 'heads',...]
    pallas_call x0 -> x1, Pallas kernels: none -> 112 us  [local_block(): pl.pallas_call(local_kernel, grid=(steps,), in_specs=[pl.BlockSpec(memory...]
    reduce_scatter x5 -> x2, waiting for transfers between devices: 187 us -> 90.7 us  [gathered_block(): lax.psum_scatter(lax.psum_scatter(part, 'heads', scatter_dimension=1), 'w...]
    reduce_sum x27 -> x5, other arithmetic: 52.1 us -> 3.3 us  [gathered_block(): squares = jnp.sum(jnp.stack([jnp.sum(entry * entry) for entry in grads]))]
    all_gather x3 -> x1, blocking collectives: 67.5 us -> 39.8 us  [gathered_block(): gains = lax.all_gather(norm_gains, both, axis=1, tiled=True)]
    unnamed x3 -> x2, blocking collectives: 104 us -> 77.2 us
  transfers between devices with their start and end apart: 11 -> 7, of which waited for: 5 -> 6; matrix products, arithmetic and copies ran while one was open for 52% -> 2% of each run, Pallas kernels for 0% -> 0%
where the time goes in v1:
time: 948 us; the launch traced here: 937 us
  waiting for transfers between devices  612 us (65%)
  blocking collectives  157 us (17%)
  Pallas kernels  112 us (12%)
  between operations  22 us (2%)
  other arithmetic  20.8 us (2%)
  local copies, waits for them, and re-layouts  13.5 us (1%)
    unnamed x8, waiting for transfers between devices  322 us
    pallas_call x1, Pallas kernels, local_block(): pl.pallas_call(local_kernel, grid=(steps,), in_specs=[pl.BlockSpec(memory...  112 us
    all_gather x2, waiting for transfers between devices, gathered_block(): lax.all_gather(lax.all_gather(own, 'wide', axis=1, tiled=True), 'heads',...  102 us
    all_gather x2, waiting for transfers between devices, gathered_block(): lax.all_gather(own, 'wide', axis=1, tiled=True)  97.5 us
    reduce_scatter x2, waiting for transfers between devices, gathered_block(): lax.psum_scatter(lax.psum_scatter(part, 'heads', scatter_dimension=1), 'w...  90.7 us
    unnamed x2, blocking collectives  77.2 us
    all_gather x1, blocking collectives, gathered_block(): gains = lax.all_gather(norm_gains, both, axis=1, tiled=True)  39.8 us
    psum x1, blocking collectives, gathered_block(): return (block_output, token_gradient, grads, lax.psum(squares, both))  39.5 us
  transfers between devices with their start and end apart: 7, of which 6 were waited for; matrix products, arithmetic and copies ran while one was open for 2% of the time, Pallas kernels for 0%

profile of v1, /device:TPU:0, one launch (start us, length us, event | category | flops | bytes accessed | tf_op | source)
XLA Modules:
  0.0 936.9 jit_solution(17709088250106987331)
XLA Ops:
  7.3 1.0 convert_element_type.27
  8.3 0.1 copy.76
  8.4 0.1 reshape.125
  8.5 0.9 bitcast_bitcast_fusion.1
  9.4 0.7 pad_maximum_fusion.1
  10.1 0.0 all-gather.10.cloned.1.call-start
  10.1 1.0 convert_element_type.29
  11.1 0.1 reshape.127
  11.2 1.0 convert_bitcast_fusion
  12.2 0.1 reshape.128
  12.3 0.2 pad_maximum_fusion
  12.5 0.8 copy.78
  13.4 42.5 %all-gather.8.cloned.1.call-done = bf16[3,768,512]{2,1,0:T(8,128)(2,1)} async-done(((bf16[3,48,512]{2,1,0:T(8,128)(2,1)}), bf16[3,768,512]{2,1,0:T(8,128)(2,1)}) %all-gather.8.cloned.1.call-update) | async-done | bytes 2359312 | tf_op jit(solution)/shard_map/all_gather | solution.py:345
  56.0 55.0 %all-gather.10.cloned.1.call-done = bf16[3,768,1024]{2,1,0:T(8,128)(2,1)} async-done(((bf16[3,48,1024]{2,1,0:T(8,128)(2,1)}), bf16[3,768,1024]{2,1,0:T(8,128)(2,1)}) %all-gather.10.cloned.1.call-update) | async-done | bytes 4718608 | tf_op jit(solution)/shard_map/all_gather | solution.py:345
  111.1 39.8 %all-gather.2 = f32[32,24,3]{1,2,0:T(4,128)S(1)} all-gather(f32[1,24,3]{1,2,0:T(4,128)S(1)} %bitcast.86), channel_id=1, replica_groups=mesh['heads'=2,'wide'=16] {'heads','wide'}, dimensions={0}, use_global_device_ids=true | all-gather | bytes 9504 | tf_op jit(solution)/shard_map/all_gather | solution.py:342
  150.9 0.7 reshape.136
  151.6 0.2 dynamic-update-slice
  151.8 37.3 %all-reduce = bf16[3072]{0:T(1024)(128)(2,1)S(1)} all-reduce(bf16[3072]{0:T(1024)(128)(2,1)S(1)} %dynamic-update-slice), channel_id=1, replica_groups=mesh['heads'=2,'wide'=16] {'heads','wide'}, use_global_device_ids=true, to_apply=%add | all-reduce | flops 3072 | bytes 12288
  189.1 0.6 broadcast_in_dim.15
  190.4 102.2 %all-gather.14.cloned.1.call-done = bf16[3,1536,1024]{2,1,0:T(8,128)(2,1)} async-done(((bf16[3,768,1024]{2,1,0:T(8,128)(2,1)}), bf16[3,1536,1024]{2,1,0:T(8,128)(2,1)}) %all-gather.14.cloned.1.call-update) | async-done | bytes 9437200 | tf_op jit(solution)/shard_map/all_gather | solution.py:344
  292.7 111.7 %local_block.1 = (f32[1024,768]{1,0:T(8,128)}, f32[1024,768]{1,0:T(8,128)}, bf16[3,2,768,512]{3,2,1,0:T(8,128)(2,1)}, bf16[3,2,768,1024]{3,2,1,0:T(8,128)(2,1)}, f32[1,3072]{1,0:T(1,128)}, /*index=5*/f32[3,768]{1,0:T(4,128)}) custom-call(s32[1]{0:T(128)S(6)} %copy.99.length_ref, bf16[1024,768]{1,0:T(8,128)(2,1)} %bitcast.73, bf16[1024,768]{1,0:T(8,128)(2,1)} %bitcast.74, ...), custom_call_target="tpu_custom_call" | custom-call | tf_op jit(solution)/shard_map/local_block/pallas_call | solution.py:278
  404.4 0.0 reduce-scatter.10.cloned.1.call-start
  404.5 0.6 copy-done.20
  405.1 0.6 dynamic-slice
  405.6 321.5 %all-reduce.9.cloned.1.call-done = (bf16[3,2,768,512]{3,2,1,0:T(8,128)(2,1)}, bf16[3,2,768,1024]{3,2,1,0:T(8,128)(2,1)}) async-done(((bf16[3,2,768,512]{3,2,1,0:T(8,128)(2,1)}, bf16[3,2,768,1024]{3,2,1,0:T(8,128)(2,1)}), (bf16[3,2,768,512]{3,2,1,0:T(8,128)(2,1)}, bf16[3,2,768,1024]{3,2,1,0:T(8,128)(2,1)})) %all-reduce.9.cloned.1.call-update) | async-done | bytes 14155792
  727.2 3.9 dynamic-slice_bitcast_fusion.1
  731.0 0.0 reduce-scatter.12.cloned.1.call-start
  731.1 5.7 dynamic-slice_bitcast_fusion
  737.8 39.9 %all-reduce.5 = (f32[3072]{0:T(1024)S(1)}, f32[3,768]{1,0:T(4,128)S(1)}) all-reduce(f32[3072]{0:T(1024)S(1)} %bitcast.85, f32[3,768]{1,0:T(4,128)S(1)} %copy-done.12), channel_id=8, replica_groups=mesh['heads'=2,'wide'=16] {'heads','wide'}, use_global_device_ids=true, to_apply=%region_8.0.clone | all-reduce | flops 5376 | bytes 43008
  777.7 0.7 multiply_reduce_fusion.5
  778.4 0.7 multiply_reduce_fusion.4
  779.1 15.2 %reduce-scatter.10.cloned.1.call-done = bf16[3,48,512]{2,1,0:T(8,128)(2,1)} async-done(((bf16[3,768,512]{2,1,0:T(8,128)(2,1)}), bf16[3,48,512]{2,1,0:T(8,128)(2,1)}) %reduce-scatter.10.cloned.1.call-update) | async-done | bytes 147472 | tf_op jit(solution)/shard_map/reduce_scatter | solution.py:350
  794.3 0.9 convert_element_type.31
  795.3 0.6 multiply_reduce_fusion.3
  795.9 0.7 multiply_reduce_fusion.2
  797.8 75.5 %reduce-scatter.12.cloned.1.call-done = bf16[3,48,1024]{2,1,0:T(8,128)(2,1)} async-done(((bf16[3,768,1024]{2,1,0:T(8,128)(2,1)}), bf16[3,48,1024]{2,1,0:T(8,128)(2,1)}) %reduce-scatter.12.cloned.1.call-update) | async-done | bytes 294928 | tf_op jit(solution)/shard_map/reduce_scatter | solution.py:350
  873.3 1.0 convert_element_type.32
  874.3 0.7 multiply_reduce_fusion
  877.6 39.5 %psum.7 = f32[]{:T(128)} all-reduce(f32[]{:T(128)S(6)} %reduce_sum.83), channel_id=1, replica_groups=mesh['heads'=2,'wide'=16] {'heads','wide'}, use_global_device_ids=true, to_apply=%region_12.0 | all-reduce | flops 1 | bytes 8 | tf_op jit(solution)/shard_map/psum | solution.py:359
  918.0 0.1 mul.386
  918.1 0.2 copy.79
  918.2 0.1 mul.388
  918.5 1.8 multiply_add_fusion.6
  920.3 1.4 multiply_add_fusion.8
  921.7 1.4 multiply_add_fusion.10
  923.1 2.2 multiply_add_fusion.4
  925.3 1.2 multiply_add_fusion
  926.4 2.3 multiply_add_fusion.2
  (61 shorter events, 0.6 us)
Async XLA Ops:
  7.2 48.7 %all-gather.8.cloned.1.call-start = ((), (), s32[]{:S(2)}) async-start(), calls=%async_computation.2 | async-start | bytes 2506752 | tf_op jit(solution)/shard_map/all_gather | solution.py:345
  10.1 100.9 %all-gather.10.cloned.1.call-start = ((), (), s32[]{:S(2)}) async-start(), calls=%async_computation.3 | async-start | bytes 5013504 | tf_op jit(solution)/shard_map/all_gather | solution.py:345
  11.2 99.8 %copy-start.13 = (f32[3,24]{1,0:T(4,128)S(1)}, f32[3,24]{1,0:T(4,128)}, u32[]{:S(2)}) copy-start(f32[3,24]{1,0:T(4,128)} %param.37) | copy-start | bytes 868
  12.2 139.4 %copy-start.18 = (f32[96]{0:T(128)S(1)}, f32[96]{0:T(128)}, u32[]{:S(2)}) copy-start(f32[96]{0:T(128)} %param.36) | copy-start | bytes 1156
  13.4 177.0 %all-gather.12.cloned.1.call-start = ((), (), s32[]{:S(2)}) async-start(), calls=%async_computation.6 | async-start | bytes 7077888 | tf_op jit(solution)/shard_map/all_gather | solution.py:344
  55.9 236.8 %all-gather.14.cloned.1.call-start = ((), (), s32[]{:S(2)}) async-start(), calls=%async_computation.7 | async-start | bytes 14155776 | tf_op jit(solution)/shard_map/all_gather | solution.py:344
  111.0 616.2 %all-reduce.9.cloned.1.call-start = ((), (), s32[]{:S(2)}) async-start(), calls=%async_computation.8 | async-start | bytes 28311552
  404.4 0.7 copy-start.20
  404.4 389.9 %reduce-scatter.10.cloned.1.call-start = ((), (), s32[]{:S(2)}) async-start(), calls=%async_computation.4 | async-start | bytes 2506752 | tf_op jit(solution)/shard_map/reduce_scatter | solution.py:350
  731.0 142.3 %reduce-scatter.12.cloned.1.call-start = ((), (), s32[]{:S(2)}) async-start(), calls=%async_computation.5 | async-start | bytes 5013504 | tf_op jit(solution)/shard_map/reduce_scatter | solution.py:350
  736.8 0.9 copy-start.11
  736.8 1.0 copy-start.12
  736.8 181.6 %copy-start.9 = (f32[384,48]{0,1:T(8,128)S(1)}, f32[384,48]{0,1:T(8,128)}, u32[]{:S(2)}) copy-start(f32[384,48]{0,1:T(8,128)} %param.33) | copy-start | bytes 221188
  736.8 181.6 %copy-start.10 = (f32[384,48]{0,1:T(8,128)S(1)}, f32[384,48]{0,1:T(8,128)}, u32[]{:S(2)}) copy-start(f32[384,48]{0,1:T(8,128)} %param.51) | copy-start | bytes 221188
  736.9 183.4 %copy-start.14 = (f32[3,24]{1,0:T(4,128)S(1)}, f32[3,24]{1,0:T(4,128)}, u32[]{:S(2)}) copy-start(f32[3,24]{1,0:T(4,128)} %param.55) | copy-start | bytes 868
  736.9 183.4 %copy-start.15 = (f32[3,24]{1,0:T(4,128)S(1)}, f32[3,24]{1,0:T(4,128)}, u32[]{:S(2)}) copy-start(f32[3,24]{1,0:T(4,128)} %param.49) | copy-start | bytes 868
  736.9 183.4 %copy-start.16 = (f32[3,24]{1,0:T(4,128)S(1)}, f32[3,24]{1,0:T(4,128)}, u32[]{:S(2)}) copy-start(f32[3,24]{1,0:T(4,128)} %param.43) | copy-start | bytes 868
  736.9 186.2 %copy-start.4 = (f32[3,48,384]{2,1,0:T(8,128)S(1)}, f32[3,48,384]{2,1,0:T(8,128)}, u32[]{:S(2)}) copy-start(f32[3,48,384]{2,1,0:T(8,128)} %param.32) | copy-start | bytes 663556
  777.7 140.1 %copy-start.17 = (f32[3,768]{1,0:T(4,128)}, f32[3,768]{1,0:T(4,128)S(1)}, u32[]{:S(2)}) copy-start(f32[3,768]{1,0:T(4,128)S(1)} %get-tuple-element.48) | copy-start | bytes 27652
  777.7 140.1 %copy-start.19 = (f32[3072]{0:T(1024)}, f32[3072]{0:T(1024)S(1)}, u32[]{:S(2)}) copy-start(f32[3072]{0:T(1024)S(1)} %get-tuple-element.47) | copy-start | bytes 36868
  779.1 146.2 %copy-start = (f32[1536,48]{0,1:T(8,128)S(1)}, f32[1536,48]{0,1:T(8,128)}, u32[]{:S(2)}) copy-start(f32[1536,48]{0,1:T(8,128)} %param.35) | copy-start | bytes 884740
  779.1 146.2 %copy-start.6 = (f32[1536,48]{0,1:T(8,128)S(1)}, f32[1536,48]{0,1:T(8,128)}, u32[]{:S(2)}) copy-start(f32[1536,48]{0,1:T(8,128)} %param.53) | copy-start | bytes 884740
  779.1 146.2 %copy-start.7 = (f32[1536,48]{0,1:T(8,128)S(1)}, f32[1536,48]{0,1:T(8,128)}, u32[]{:S(2)}) copy-start(f32[1536,48]{0,1:T(8,128)} %param.47) | copy-start | bytes 884740
  779.1 146.2 %copy-start.8 = (f32[1536,48]{0,1:T(8,128)S(1)}, f32[1536,48]{0,1:T(8,128)}, u32[]{:S(2)}) copy-start(f32[1536,48]{0,1:T(8,128)} %param.41) | copy-start | bytes 884740
  917.9 8.5 copy-start.1
  918.4 10.4 %copy-start.5 = (f32[3,48,384]{2,1,0:T(8,128)}, f32[3,48,384]{2,1,0:T(8,128)S(1)}, u32[]{:S(2)}) copy-start(f32[3,48,384]{2,1,0:T(8,128)S(1)} %mul.388) | copy-start | bytes 663556
  918.4 10.4 %copy-start.2 = (f32[3,6,8,512]{3,2,0,1:T(8,128)}, f32[3,6,8,512]{3,2,0,1:T(8,128)S(1)}, u32[]{:S(2)}) copy-start(f32[3,6,8,512]{3,2,0,1:T(8,128)S(1)} %copy.92) | copy-start | bytes 884740
  918.4 10.3 %copy-start.3 = (f32[3,6,8,512]{3,2,0,1:T(8,128)}, f32[3,6,8,512]{3,2,0,1:T(8,128)S(1)}, u32[]{:S(2)}) copy-start(f32[3,6,8,512]{3,2,0,1:T(8,128)S(1)} %copy.91) | copy-start | bytes 884740
Sparse Core Ops, SparseCore 0:
  10.9 44.9 all-gather.7
  58.7 52.1 all-gather.9
  112.5 61.8 all-gather.11
  175.9 116.7 all-gather.13
  404.6 322.5 all-reduce.8
  731.2 63.1 reduce-scatter.9
  798.7 74.5 reduce-scatter.11
